TPU v7x, 256 devices: a whole 4x4x8 slice. The times are simulated.
256 devices in a mesh: dom: 32 (over z, y), batch: 8 (over x, core).
Axes of the slice: x: 4, y: 4, z: 8, core: 2. Of those that a mesh axis runs over, the one named last changes fastest.
Arguments:
- activations: bfloat16 [2048, 65536], P('batch', 'dom'), may hold values from 0 to 2
- tile_weights: bfloat16 [4, 512, 512, 128], P(None, 'dom', 'batch'), may hold values from -0.375 to 0.375
- biases: float32 [4, 65536], P(None, 'dom'), may hold values from -2.5 to 2.5
- source_codes: int32 [4, 512, 4], P(None, 'dom'), may hold values from 0 to 19
- send_list: int32 [4, 32, 4], P(None, 'dom'), may hold values from 0 to 15
Outputs:
- result: bfloat16 [2048, 65536], P('batch', 'dom')
All inputs are finite; a program needn't handle non-finite values.
Results may differ from a plain program's by a relative error of at most 0.0062.
Values may be sent and summed in bfloat16 or wider, within the bound.
A program may use at most 64 MiB of HBM per device.

v0:
```python
import jax
import jax.numpy as jnp
from jax import lax
from jax.sharding import PartitionSpec as P


def body(activations, tile_weights, biases, source_codes, send_list):
    row_count = activations.shape[0]
    tile_width = tile_weights.shape[3]
    block_count = source_codes.shape[1]
    fan_tiles = source_codes.shape[2]
    layer_count = tile_weights.shape[0]
    part_count = lax.axis_size("dom")
    own_index = lax.axis_index("dom")
    neighbor_offsets = (1, 2, -1, part_count // 2)
    offset_table = jnp.array(neighbor_offsets, jnp.int32)
    senders = (own_index - offset_table) % part_count
    destinations = (own_index + offset_table) % part_count
    current = activations.reshape(row_count, block_count, tile_width)
    for layer_index in range(layer_count):
        outgoing = jnp.take(current, send_list[layer_index, 0], axis=1)
        one_hot = (jnp.arange(part_count)[:, None] == destinations[None, :]).astype(jnp.bfloat16)
        out_blocks = jnp.einsum(
            "qn,rnc->qrc", one_hot, outgoing, preferred_element_type=jnp.float32
        ).astype(jnp.bfloat16)
        in_blocks = lax.all_to_all(out_blocks, "dom", split_axis=0, concat_axis=0, tiled=True)
        arrived = jnp.transpose(jnp.take(in_blocks, senders, axis=0), (1, 0, 2))
        block_pool = jnp.concatenate([current, arrived], axis=1)
        input_panel = jnp.take(block_pool, source_codes[layer_index].reshape(-1), axis=1)
        input_panel = input_panel.reshape(row_count, block_count, fan_tiles * tile_width)
        layer_bias = biases[layer_index].reshape(block_count, tile_width)
        summed = jnp.einsum(
            "rjc,jco->rjo",
            input_panel,
            lax.all_gather(tile_weights[layer_index], "batch", axis=1, tiled=True),
            preferred_element_type=jnp.float32,
        )
        current = jnp.maximum(summed + layer_bias[None], 0.0).astype(jnp.bfloat16)
    return current.reshape(row_count, block_count * tile_width)


def solution(mesh):
    in_specs = (
        P("batch", "dom"),
        P(None, "dom", "batch", None),
        P(None, "dom"),
        P(None, "dom", None),
        P(None, "dom", None),
    )
    out_specs = P("batch", "dom")
    return jax.shard_map(body, mesh=mesh, in_specs=in_specs, out_specs=out_specs, check_vma=False)
```

profile of v0, /device:TPU:1, one launch (start us, length us, event | category | flops | bytes accessed | tf_op | source)
XLA Modules:
  0.0 332.8 jit_solution(4580243394682207343)
XLA Ops:
  6.5 0.7 compare_and_fusion.1
  7.3 1.5 copy.71
  8.8 0.7 copy.75
  9.4 0.6 gather_fusion
  10.0 0.1 select_bitcast_fusion.11
  10.2 0.8 convolution_convert_fusion.3
  11.0 2.1 copy.74
  13.1 12.3 %all-to-all-start = ((bf16[32,256,128]{2,1,0:T(8,128)(2,1)}), bf16[32,256,128]{2,1,0:T(8,128)(2,1)}, u32[]{:S(2)}, u32[]{:S(2)}) async-start(bf16[32,256,128]{2,1,0:T(8,128)(2,1)} %copy.74), calls=%async_computation | async-start | bytes 4194304 | tf_op jit(solution)/shard_map/all_to_all | solution.py:26
  25.5 1.0 fusion.39
  26.9 47.0 %all-to-all-done = bf16[32,256,128]{2,1,0:T(8,128)(2,1)} async-done(((bf16[32,256,128]{2,1,0:T(8,128)(2,1)}), bf16[32,256,128]{2,1,0:T(8,128)(2,1)}, u32[]{:S(2)}, u32[]{:S(2)}) %all-to-all-start) | async-done | bytes 2097184 | tf_op jit(solution)/shard_map/all_to_all | solution.py:26
  73.9 2.2 gather_fusion.1
  76.1 0.1 select_bitcast_fusion.10
  76.2 0.1 pad_maximum_fusion
  76.3 3.1 gather_fusion.2
  79.4 4.6 %select_bitcast_fusion.3 = bf16[256,64,128]{2,0,1:T(8,128)(2,1)} fusion(bf16[64,256,128]{2,1,0:T(8,128)(2,1)} %gather_fusion.2, pred[64]{0:T(512)(128)(4,1)S(1)} %compare_and_fusion.6), kind=kLoop, calls=%fused_computation.15 | loop fusion | flops 2097152 | bytes 8388672 | tf_op jit(solution)/shard_map/jit(_take)/select_n | solution.py:29
  84.0 6.4 %copy.76 = bf16[256,64,128]{0,2,1:T(8,128)(2,1)} copy(bf16[256,64,128]{2,0,1:T(8,128)(2,1)} %select_bitcast_fusion.3) | data formatting | bytes 8388608 | tf_op jit(solution)/shard_map/jit(_take)/select_n | solution.py:29
  90.4 4.2 %fusion.16 = bf16[256,16,128]{2,0,1:T(8,128)(2,1)S(1)} fusion(bf16[256,16,512]{0,2,1:T(8,128)(2,1)} %bitcast.92, bf16[1,16,512,128]{3,2,1,0:T(8,128)(2,1)} %all-gather.9.cloned.1.call-done, f32[16,128]{1,0:T(8,128)S(1)} %bitcast.101), kind=kOutput, calls=%fused_computation.32 | convolution fusion | flops 538443776 | bytes 7348224 | tf_op jit(solution)/shard_map/rjc,jco->rjo/dot_general | solution.py:32
  94.7 0.6 gather_fusion.3
  95.3 0.1 select_bitcast_fusion.9
  95.4 0.8 convolution_convert_fusion.2
  96.2 2.2 copy.79
  98.4 6.7 %all-to-all-start.1 = ((bf16[32,256,128]{2,1,0:T(8,128)(2,1)}), bf16[32,256,128]{2,1,0:T(8,128)(2,1)S(1)}, u32[]{:S(2)}, u32[]{:S(2)}) async-start(bf16[32,256,128]{2,1,0:T(8,128)(2,1)} %copy.79), calls=%async_computation.1 | async-start | bytes 4194304 | tf_op jit(solution)/shard_map/all_to_all | solution.py:26
  105.0 0.2 all-gather.11.cloned.1.call-start
  105.3 0.5 all-gather.11.cloned.1.call-update
  106.0 46.4 %all-to-all-done.1 = bf16[32,256,128]{2,1,0:T(8,128)(2,1)S(1)} async-done(((bf16[32,256,128]{2,1,0:T(8,128)(2,1)}), bf16[32,256,128]{2,1,0:T(8,128)(2,1)S(1)}, u32[]{:S(2)}, u32[]{:S(2)}) %all-to-all-start.1) | async-done | bytes 2097184 | tf_op jit(solution)/shard_map/all_to_all | solution.py:26
  152.4 0.6 gather_fusion.4
  153.0 0.1 select_bitcast_fusion.8
  153.1 0.1 pad_maximum_fusion.1
  153.2 3.1 gather_fusion.5
  156.3 4.6 %select_bitcast_fusion.2 = bf16[256,64,128]{2,0,1:T(8,128)(2,1)} fusion(bf16[64,256,128]{2,1,0:T(8,128)(2,1)} %gather_fusion.5, pred[64]{0:T(512)(128)(4,1)S(1)} %compare_and_fusion.4), kind=kLoop, calls=%fused_computation.14 | loop fusion | flops 2097152 | bytes 8388672 | tf_op jit(solution)/shard_map/jit(_take)/select_n | solution.py:29
  161.0 6.4 %copy.80 = bf16[256,64,128]{0,2,1:T(8,128)(2,1)} copy(bf16[256,64,128]{2,0,1:T(8,128)(2,1)} %select_bitcast_fusion.2) | data formatting | bytes 8388608 | tf_op jit(solution)/shard_map/jit(_take)/select_n | solution.py:29
  167.3 4.2 %fusion.19 = bf16[256,16,128]{2,0,1:T(8,128)(2,1)S(1)} fusion(bf16[256,16,512]{0,2,1:T(8,128)(2,1)} %bitcast.93, bf16[1,16,512,128]{3,2,1,0:T(8,128)(2,1)} %all-gather.11.cloned.1.call-done, f32[16,128]{1,0:T(8,128)S(1)} %bitcast.100), kind=kOutput, calls=%fused_computation.33 | convolution fusion | flops 538443776 | bytes 7348224 | tf_op jit(solution)/shard_map/rjc,jco->rjo/dot_general | solution.py:32
  171.6 0.6 gather_fusion.6
  172.2 0.1 select_bitcast_fusion.7
  172.3 0.8 convolution_convert_fusion.1
  173.1 2.2 copy.83
  175.3 7.2 %all-to-all-start.2 = ((bf16[32,256,128]{2,1,0:T(8,128)(2,1)}), bf16[32,256,128]{2,1,0:T(8,128)(2,1)S(1)}, u32[]{:S(2)}, u32[]{:S(2)}) async-start(bf16[32,256,128]{2,1,0:T(8,128)(2,1)} %copy.83), calls=%async_computation.2 | async-start | bytes 4194304 | tf_op jit(solution)/shard_map/all_to_all | solution.py:26
  182.6 0.7 all-gather.13.cloned.1.call-update
  183.5 45.3 %all-to-all-done.2 = bf16[32,256,128]{2,1,0:T(8,128)(2,1)S(1)} async-done(((bf16[32,256,128]{2,1,0:T(8,128)(2,1)}), bf16[32,256,128]{2,1,0:T(8,128)(2,1)S(1)}, u32[]{:S(2)}, u32[]{:S(2)}) %all-to-all-start.2) | async-done | bytes 2097184 | tf_op jit(solution)/shard_map/all_to_all | solution.py:26
  228.8 0.6 gather_fusion.7
  229.4 0.1 select_bitcast_fusion.6
  229.5 0.1 pad_maximum_fusion.2
  229.6 3.1 gather_fusion.8
  232.7 4.6 %select_bitcast_fusion.1 = bf16[256,64,128]{2,0,1:T(8,128)(2,1)} fusion(bf16[64,256,128]{2,1,0:T(8,128)(2,1)} %gather_fusion.8, pred[64]{0:T(512)(128)(4,1)S(1)} %compare_and_fusion.2), kind=kLoop, calls=%fused_computation.13 | loop fusion | flops 2097152 | bytes 8388672 | tf_op jit(solution)/shard_map/jit(_take)/select_n | solution.py:29
  237.4 6.4 %copy.84 = bf16[256,64,128]{0,2,1:T(8,128)(2,1)} copy(bf16[256,64,128]{2,0,1:T(8,128)(2,1)} %select_bitcast_fusion.1) | data formatting | bytes 8388608 | tf_op jit(solution)/shard_map/jit(_take)/select_n | solution.py:29
  243.7 4.2 %fusion.22 = bf16[256,16,128]{2,0,1:T(8,128)(2,1)S(1)} fusion(bf16[256,16,512]{0,2,1:T(8,128)(2,1)} %bitcast.94, bf16[1,16,512,128]{3,2,1,0:T(8,128)(2,1)} %all-gather.13.cloned.1.call-done, f32[16,128]{1,0:T(8,128)S(1)} %bitcast.99), kind=kOutput, calls=%fused_computation.34 | convolution fusion | flops 538443776 | bytes 7348224 | tf_op jit(solution)/shard_map/rjc,jco->rjo/dot_general | solution.py:32
  248.0 0.6 gather_fusion.9
  248.6 0.1 select_bitcast_fusion.5
  248.7 0.8 convolution_convert_fusion
  249.5 2.2 copy.87
  251.7 7.5 %all-to-all-start.3 = ((bf16[32,256,128]{2,1,0:T(8,128)(2,1)}), bf16[32,256,128]{2,1,0:T(8,128)(2,1)S(1)}, u32[]{:S(2)}, u32[]{:S(2)}) async-start(bf16[32,256,128]{2,1,0:T(8,128)(2,1)} %copy.87), calls=%async_computation.3 | async-start | bytes 4194304 | tf_op jit(solution)/shard_map/all_to_all | solution.py:26
  259.2 0.3 all-gather.15.cloned.1.call-start
  259.5 0.9 copy.100
  260.6 33.2 %all-gather.15.cloned.1.call-done = bf16[1,16,512,128]{3,1,0,2:T(8,128)(2,1)} async-done(((bf16[1,16,64,128]{3,1,0,2:T(8,128)(2,1)}), bf16[1,16,512,128]{3,1,0,2:T(8,128)(2,1)}) %all-gather.15.cloned.1.call-update) | async-done | bytes 2097168 | tf_op jit(solution)/shard_map/all_gather | solution.py:35
  293.8 4.4 %copy.90 = bf16[1,16,512,128]{2,3,1,0:T(8,128)(2,1)} copy(bf16[1,16,512,128]{3,1,0,2:T(8,128)(2,1)} %all-gather.15.cloned.1.call-done) | data formatting | bytes 4194304 | tf_op jit(solution)/shard_map/all_gather | solution.py:35
  298.2 7.4 %all-to-all-done.3 = bf16[32,256,128]{2,1,0:T(8,128)(2,1)S(1)} async-done(((bf16[32,256,128]{2,1,0:T(8,128)(2,1)}), bf16[32,256,128]{2,1,0:T(8,128)(2,1)S(1)}, u32[]{:S(2)}, u32[]{:S(2)}) %all-to-all-start.3) | async-done | bytes 2097184 | tf_op jit(solution)/shard_map/all_to_all | solution.py:26
  305.6 0.6 gather_fusion.10
  306.3 0.1 pad_maximum_fusion.3
  306.5 3.1 gather_fusion.11
  309.6 4.6 %select_bitcast_fusion = bf16[256,64,128]{2,0,1:T(8,128)(2,1)} fusion(bf16[64,256,128]{2,1,0:T(8,128)(2,1)} %gather_fusion.11, pred[64]{0:T(512)(128)(4,1)S(1)} %compare_and_fusion), kind=kLoop, calls=%fused_computation.12 | loop fusion | flops 2097152 | bytes 8388672 | tf_op jit(solution)/shard_map/jit(_take)/select_n | solution.py:29
  314.2 6.5 %copy.88 = bf16[256,64,128]{0,2,1:T(8,128)(2,1)} copy(bf16[256,64,128]{2,0,1:T(8,128)(2,1)} %select_bitcast_fusion) | data formatting | bytes 8388608 | tf_op jit(solution)/shard_map/jit(_take)/select_n | solution.py:29
  320.7 3.6 %fusion.25 = bf16[256,16,128]{2,0,1:T(8,128)(2,1)S(1)} fusion(bf16[256,16,512]{0,2,1:T(8,128)(2,1)} %bitcast.95, bf16[1,16,512,128]{2,3,1,0:T(8,128)(2,1)S(1)} %copy-done, f32[16,128]{1,0:T(8,128)S(1)} %bitcast.98), kind=kOutput, calls=%fused_computation.35 | convolution fusion | flops 538443776 | bytes 7348224 | tf_op jit(solution)/shard_map/rjc,jco->rjo/dot_general | solution.py:32
  324.3 0.5 copy.93
  324.8 1.4 copy.94
  (51 shorter events, 1.1 us)
Async XLA Ops:
  8.8 1.4 copy-start.6
  13.1 12.4 %copy-start.1 = (bf16[4,16,64,128]{3,2,1,0:T(8,128)(2,1)S(1)}, bf16[4,16,64,128]{3,2,1,0:T(8,128)(2,1)}, u32[]{:S(2)}) copy-start(bf16[4,16,64,128]{3,2,1,0:T(8,128)(2,1)} %param.13) | copy-start | bytes 3145732
  13.1 60.7 %all-to-all-start = ((bf16[32,256,128]{2,1,0:T(8,128)(2,1)}), bf16[32,256,128]{2,1,0:T(8,128)(2,1)}, u32[]{:S(2)}, u32[]{:S(2)}) async-start(bf16[32,256,128]{2,1,0:T(8,128)(2,1)} %copy.74), calls=%async_computation | async-start | bytes 4194304 | tf_op jit(solution)/shard_map/all_to_all | solution.py:26
  25.4 1.1 copy-start.4
  25.4 1.3 copy-start.5
  25.5 1.4 copy-start.3
  25.5 64.9 %all-gather.9.cloned.1.call-start = ((), (), s32[]{:S(2)}) async-start(), calls=%async_computation.4 | async-start | bytes 2359296 | tf_op jit(solution)/shard_map/all_gather | solution.py:35
  98.4 54.0 %all-to-all-start.1 = ((bf16[32,256,128]{2,1,0:T(8,128)(2,1)}), bf16[32,256,128]{2,1,0:T(8,128)(2,1)S(1)}, u32[]{:S(2)}, u32[]{:S(2)}) async-start(bf16[32,256,128]{2,1,0:T(8,128)(2,1)} %copy.79), calls=%async_computation.1 | async-start | bytes 4194304 | tf_op jit(solution)/shard_map/all_to_all | solution.py:26
  105.0 62.3 %all-gather.11.cloned.1.call-start = ((), (), s32[]{:S(2)}) async-start(), calls=%async_computation.5 | async-start | bytes 2359296 | tf_op jit(solution)/shard_map/all_gather | solution.py:35
  175.3 53.5 %all-to-all-start.2 = ((bf16[32,256,128]{2,1,0:T(8,128)(2,1)}), bf16[32,256,128]{2,1,0:T(8,128)(2,1)S(1)}, u32[]{:S(2)}, u32[]{:S(2)}) async-start(bf16[32,256,128]{2,1,0:T(8,128)(2,1)} %copy.83), calls=%async_computation.2 | async-start | bytes 4194304 | tf_op jit(solution)/shard_map/all_to_all | solution.py:26
  182.5 61.2 %all-gather.13.cloned.1.call-start = ((), (), s32[]{:S(2)}) async-start(), calls=%async_computation.6 | async-start | bytes 2359296 | tf_op jit(solution)/shard_map/all_gather | solution.py:35
  251.7 7.8 %copy-start.2 = (bf16[1,16,64,128]{3,2,1,0:T(8,128)(2,1)S(1)}, bf16[1,16,64,128]{3,2,1,0:T(8,128)(2,1)}, u32[]{:S(2)}) copy-start(bf16[1,16,64,128]{3,2,1,0:T(8,128)(2,1)} %get-tuple-element.18) | copy-start | bytes 786436
  251.7 53.9 %all-to-all-start.3 = ((bf16[32,256,128]{2,1,0:T(8,128)(2,1)}), bf16[32,256,128]{2,1,0:T(8,128)(2,1)S(1)}, u32[]{:S(2)}, u32[]{:S(2)}) async-start(bf16[32,256,128]{2,1,0:T(8,128)(2,1)} %copy.87), calls=%async_computation.3 | async-start | bytes 4194304 | tf_op jit(solution)/shard_map/all_to_all | solution.py:26
  259.2 34.6 %all-gather.15.cloned.1.call-start = ((), (), s32[]{:S(2)}) async-start(), calls=%async_computation.7 | async-start | bytes 2359296 | tf_op jit(solution)/shard_map/all_gather | solution.py:35
  314.2 6.5 %copy-start = (bf16[1,16,512,128]{2,3,1,0:T(8,128)(2,1)S(1)}, bf16[1,16,512,128]{2,3,1,0:T(8,128)(2,1)}, u32[]{:S(2)}) copy-start(bf16[1,16,512,128]{2,3,1,0:T(8,128)(2,1)} %copy.90) | copy-start | bytes 6291460
Sparse Core Ops, SparseCore 0:
  28.1 29.6 all-gather.8
  107.7 30.7 all-gather.10
  185.2 31.2 all-gather.12
  261.6 32.2 all-gather.14
where the time goes:
time: 338 us; the launch traced here: 333 us
  waiting for transfers between devices  181 us (54%)
  local copies, waits for them, and re-layouts  64 us (19%)
  starting transfers between devices  34.3 us (10%)
  other arithmetic  20.6 us (6%)
  matrix products  19.6 us (6%)
  between operations  13.6 us (4%)
    all_to_all x4, waiting for transfers between devices, body(): lax.all_to_all(out_blocks, 'dom', split_axis=0, concat_axis=0, tiled=True)  146 us
    all_to_all x4, starting transfers between devices, body(): lax.all_to_all(out_blocks, 'dom', split_axis=0, concat_axis=0, tiled=True)  33.7 us
    all_gather x4, waiting for transfers between devices, body(): lax.all_gather(tile_weights[layer_index], 'batch', axis=1, tiled=True)  33.2 us
    select_n x4, local copies, waits for them, and re-layouts, body(): jnp.take(block_pool, source_codes[layer_index].reshape(-1), axis=1)  25.6 us
    select_n x8, other arithmetic, body(): jnp.take(block_pool, source_codes[layer_index].reshape(-1), axis=1)  18.6 us
    dot_general x4, matrix products, body(): jnp.einsum('rjc,jco->rjo', input_panel, lax.all_gather(tile_weights[layer...  16.3 us
    gather x4, local copies, waits for them, and re-layouts, body(): jnp.take(block_pool, source_codes[layer_index].reshape(-1), axis=1)  12.4 us
    convert_element_type x4, local copies, waits for them, and re-layouts, body(): out_blocks = jnp.einsum('qn,rnc->qrc', one_hot, outgoing, preferred_eleme...  8.6 us
  transfers between devices with their start and end apart: 8, of which 5 were waited for; matrix products, arithmetic and copies ran while one was open for 16% of the time, Pallas kernels for 0%

commit v1 on v0

v1 whole, which is shorter than its diff:
```python
import jax
import jax.numpy as jnp
from jax import lax
from jax.experimental import pallas as pl
from jax.experimental.pallas import tpu as pltpu
from jax.sharding import PartitionSpec as P

MESH = pl.DeviceIdType.MESH
LAYERS, BLK, FAN, TILE, NEIGH = 4, 16, 4, 128, 4
CHIPS, CORES = 4, 2
SHARDS = CHIPS * CORES
HALF = BLK // 2


def kernel(parts, rows, act, weights, biases, codes, sends, out, *scratch):
    wbufs, pools, stages = scratch[0:4], scratch[4:8], scratch[8:12]
    first, final, bias_v = scratch[12:15]
    xs_send, xs_recv, pt_send, pt_recv, bd_send, bd_recv, ld_sem, out_sem = scratch[15:]

    dom = lax.axis_index("dom")
    me = lax.axis_index("batch")
    chip, core = me // CORES, me % CORES
    right = lax.rem(chip + 1, CHIPS) * CORES + core
    left = lax.rem(chip + CHIPS - 1, CHIPS) * CORES + core
    far = lax.rem(chip + 2, CHIPS) * CORES + core
    partner = chip * CORES + 1 - core
    offsets = (1, 2, parts - 1, parts // 2)

    loads = []

    def load(source, target):
        copy = pltpu.make_async_copy(source, target, ld_sem.at[len(loads)])
        copy.start()
        loads.append(copy)

    load(weights.at[0], wbufs[0].at[me])
    for j in range(BLK):
        load(act.at[:, pl.ds(j * TILE, TILE)], first.at[j])
    for l in range(1, LAYERS):
        load(weights.at[l], wbufs[l].at[me])
    for j in range(BLK):
        load(biases.at[:, pl.ds(j * TILE, TILE)], bias_v.at[j])
    for j in range(BLK):
        load(act.at[:, pl.ds(j * TILE, TILE)], pools[0].at[j])

    barrier = pltpu.get_barrier_semaphore()
    for peer in (left, right, partner):
        pl.semaphore_signal(barrier, inc=1, device_id={"batch": peer}, device_id_type=MESH)
    for offset in offsets:
        sender = lax.rem(dom + parts - offset, parts)
        pl.semaphore_signal(barrier, inc=1, device_id={"dom": sender}, device_id_type=MESH)
    pl.semaphore_wait(barrier, 7)

    started = []

    def piece(l, b, h):
        return wbufs[l].at[b, pl.ds(h * HALF, HALF)]

    def ring(l, direction, slot, b):
        half = (direction if slot != 1 else 1 - direction)
        ref = piece(l, b, half)
        return pltpu.make_async_remote_copy(
            src_ref=ref, dst_ref=ref,
            send_sem=xs_send.at[l, direction, slot], recv_sem=xs_recv.at[l, direction, slot],
            device_id={"batch": right if direction == 0 else left}, device_id_type=MESH)

    def ring_start(l, direction, slot, b):
        copy = ring(l, direction, slot, b)
        copy.start()
        started.append(copy)

    origin = ((left, left, far), (right, right, far))

    def ring_wait(l, direction, slot):
        ring(l, direction, slot, origin[direction][slot]).wait_recv()

    def hand(l, slot, ref):
        return pltpu.make_async_remote_copy(
            src_ref=ref, dst_ref=ref, send_sem=pt_send.at[l, slot], recv_sem=pt_recv.at[l, slot],
            device_id={"batch": partner}, device_id_type=MESH)

    def hand_start(l, slot, ref):
        copy = hand(l, slot, ref)
        copy.start()
        started.append(copy)

    def hand_wait(l):
        for slot in range(6):
            direction, s = slot % 2, slot // 2
            half = (direction if s != 1 else 1 - direction)
            b = origin[direction][s] + 1 - 2 * core
            hand(l, slot, piece(l, b, half)).wait_recv()
        hand(l, 6, wbufs[l].at[partner]).wait_recv()

    def boundary(l, i):
        return pltpu.make_async_remote_copy(
            src_ref=stages[l].at[i], dst_ref=pools[l].at[BLK + i],
            send_sem=bd_send.at[l, i], recv_sem=bd_recv.at[l, i],
            device_id={"dom": lax.rem(dom + offsets[i], parts)}, device_id_type=MESH)

    def boundary_start(l):
        for i in (3, 0, 1, 2):
            copy = boundary(l, i)
            copy.start()
            started.append(copy)

    def step(l, s):
        for direction in range(2):
            ring_wait(l, direction, s)
        if s == 0:
            ring_start(l, 0, 2, left)
            ring_start(l, 1, 2, right)
        elif l + 1 < LAYERS:
            for direction in range(2):
                ring_start(l + 1, direction, s - 1, me)
        for direction in range(2):
            half = (direction if s != 1 else 1 - direction)
            hand_start(l, 2 * s + direction, piece(l, origin[direction][s], half))

    def block(l, j):
        x = jnp.concatenate([pools[l][codes[l, j, k]] for k in range(FAN)], axis=1)
        w = jnp.concatenate([wbufs[l][b, j] for b in range(SHARDS)], axis=0)
        summed = jnp.dot(x, w, preferred_element_type=jnp.float32)
        return jnp.maximum(summed + bias_v[j][l:l + 1], 0.0).astype(jnp.bfloat16)

    for copy in loads[:1 + BLK]:
        copy.wait()
    for s in range(2):
        for direction in range(2):
            ring_start(0, direction, s, me)
    hand_start(0, 6, wbufs[0].at[me])
    for i in (3, 0, 1, 2):
        stages[0][i] = first[sends[0, 0, i]]
    for copy in loads[1 + BLK:]:
        copy.wait()
    boundary_start(0)
    for l in range(1, LAYERS):
        hand_start(l, 6, wbufs[l].at[me])

    for l in range(LAYERS):
        for s in range(3):
            step(l, s)
        hand_wait(l)
        for i in range(NEIGH):
            boundary(l, i).wait_recv()
        if l + 1 < LAYERS:
            for i in (3, 0, 1, 2):
                stages[l + 1][i] = block(l, sends[l + 1, 0, i])
            boundary_start(l + 1)

            @pl.loop(0, BLK)
            def _(j):
                pools[l + 1][j] = block(l, j)
        else:
            def store(j):
                columns = pl.ds(pl.multiple_of(j * TILE, TILE), TILE)
                return pltpu.make_async_copy(final.at[j], out.at[:, columns], out_sem.at[j])

            @pl.loop(0, BLK)
            def _(j):
                final[j] = block(l, j)

                @pl.when(j > 0)
                def _():
                    store(j - 1).start()

            store(BLK - 1).start()
            for j in range(BLK):
                store(j).wait()
    for copy in started:
        copy.wait_send()


def body(activations, tile_weights, biases, source_codes, send_list):
    rows = activations.shape[0]
    parts = lax.axis_size("dom")
    part_rows = FAN * TILE // SHARDS
    anywhere = pl.BlockSpec(memory_space=pl.ANY)
    scalars = pl.BlockSpec(memory_space=pltpu.SMEM)
    dma = pltpu.SemaphoreType.DMA
    return pl.pallas_call(
        lambda *refs: kernel(parts, rows, *refs),
        out_shape=jax.ShapeDtypeStruct(activations.shape, jnp.bfloat16),
        in_specs=[anywhere, anywhere, anywhere, scalars, scalars],
        out_specs=anywhere,
        scratch_shapes=(
            [pltpu.VMEM((SHARDS, BLK, part_rows, TILE), jnp.bfloat16)] * LAYERS
            + [pltpu.VMEM((BLK + NEIGH, rows, TILE), jnp.bfloat16)] * LAYERS
            + [pltpu.VMEM((NEIGH, rows, TILE), jnp.bfloat16)] * LAYERS
            + [
                pltpu.VMEM((BLK, rows, TILE), jnp.bfloat16),
                pltpu.VMEM((BLK, rows, TILE), jnp.bfloat16),
                pltpu.VMEM((BLK, LAYERS, TILE), jnp.float32),
                dma((LAYERS, 2, 3)), dma((LAYERS, 2, 3)),
                dma((LAYERS, 7)), dma((LAYERS, 7)),
                dma((LAYERS, NEIGH)), dma((LAYERS, NEIGH)),
                dma((3 * BLK + LAYERS,)), dma((BLK,)),
            ]
        ),
        compiler_params=pltpu.CompilerParams(collective_id=0, has_side_effects=True),
        name="layers",
    )(activations, tile_weights, biases, source_codes, send_list)


def solution(mesh):
    in_specs = (
        P("batch", "dom"),
        P(None, "dom", "batch", None),
        P(None, "dom"),
        P(None, "dom", None),
        P(None, "dom", None),
    )
    out_specs = P("batch", "dom")
    return jax.shard_map(body, mesh=mesh, in_specs=in_specs, out_specs=out_specs, check_vma=False)
```

time: 338 us -> 66.2 us (0.20); the launches traced: 333 us -> 65.9 us
  waiting for transfers between devices: 181 us -> 0 us
  Pallas kernels: 0 us -> 62.2 us
  local copies, waits for them, and re-layouts: 64 us -> 3.71 us
  starting transfers between devices: 34.3 us -> 0 us
  other arithmetic: 20.6 us -> 0 us
  matrix products: 19.6 us -> 0 us
  between operations: 13.6 us -> 0.01 us
    all_to_all x4 -> x0, waiting for transfers between devices: 146 us -> none  [body(): lax.all_to_all(out_blocks, 'dom', split_axis=0, concat_axis=0, tiled=True)]
    pallas_call x0 -> x1, Pallas kernels: none -> 62.2 us  [body(): pl.pallas_call(lambda *refs: kernel(parts, rows, *refs), out_shape=jax.Sh...]
    all_to_all x4 -> x0, starting transfers between devices: 33.7 us -> none  [body(): lax.all_to_all(out_blocks, 'dom', split_axis=0, concat_axis=0, tiled=True)]
    all_gather x4 -> x0, waiting for transfers between devices: 33.2 us -> none  [body(): lax.all_gather(tile_weights[layer_index], 'batch', axis=1, tiled=True)]
    select_n x4 -> x0, local copies, waits for them, and re-layouts: 25.6 us -> none  [body(): jnp.take(block_pool, source_codes[layer_index].reshape(-1), axis=1)]
    dot_general x8 -> x0, matrix products: 19.6 us -> none  [the longest x4 16.3 us: body(): jnp.einsum('rjc,jco->rjo', input_panel, lax.all_gather(tile_weights[layer...]
    select_n x13 -> x0, other arithmetic: 19 us -> none  [the longest x8 18.6 us: body(): jnp.take(block_pool, source_codes[layer_index].reshape(-1), axis=1)]
    gather x12 -> x0, local copies, waits for them, and re-layouts: 18.8 us -> none  [the longest x4 12.4 us: body(): jnp.take(block_pool, source_codes[layer_index].reshape(-1), axis=1)]
  transfers between devices with their start and end apart: 8 -> 0, of which waited for: 5 -> 0; matrix products, arithmetic and copies ran while one was open for 16% -> 0% of each run, Pallas kernels for 0% -> 0%
where the time goes in v1:
time: 66.2 us; the launch traced here: 65.9 us
  Pallas kernels  62.2 us (94%)
  local copies, waits for them, and re-layouts  3.71 us (6%)
    pallas_call x1, Pallas kernels, body(): pl.pallas_call(lambda *refs: kernel(parts, rows, *refs), out_shape=jax.Sh...  62.2 us
    unnamed x2, local copies, waits for them, and re-layouts  3.71 us

profile of v1, /device:TPU:1, one launch (start us, length us, event | category | flops | bytes accessed | tf_op | source)
XLA Modules:
  0.0 65.9 jit_solution(7295532313116015330)
XLA Ops:
  0.0 1.4 %copy.6.refs_3_ = s32[4,16,4]{2,1,0:T(8,128)} copy(s32[4,16,4]{1,2,0:T(4,128)} %param.8) | data formatting | bytes 2048 | tf_op args[3]
  1.4 62.2 %layers.1 = bf16[256,2048]{1,0:T(8,128)(2,1)} custom-call(bf16[256,2048]{1,0:T(8,128)(2,1)} %refs_0_.1, bf16[4,16,64,128]{3,2,1,0:T(8,128)(2,1)} %refs_1_.1, f32[4,2048]{1,0:T(4,128)} %refs_2_.1, s32[4,16,4]{2,1,0:T(8,128)} %copy.6.refs_3_, s32[4,1,4]{2,1,0:T(1,128)} %refs_4_.1), custom_call_target="tpu_custom_call" | custom-call | tf_op jit(solution)/shard_map/layers/pallas_call | solution.py:181
  63.6 2.3 %copy.8 = bf16[256,2048]{1,0:T(8,128)(2,1)} copy(bf16[256,2048]{1,0:T(8,128)(2,1)} %layers.1) | data formatting | bytes 2097152

commit v2 on v1

--- a/solution.py
+++ b/solution.py
@@ -10,12 +10,13 @@
 CHIPS, CORES = 4, 2
 SHARDS = CHIPS * CORES
 HALF = BLK // 2
+GROUP = 4
 
 
 def kernel(parts, rows, act, weights, biases, codes, sends, out, *scratch):
     wbufs, pools, stages = scratch[0:4], scratch[4:8], scratch[8:12]
-    first, final, bias_v = scratch[12:15]
-    xs_send, xs_recv, pt_send, pt_recv, bd_send, bd_recv, ld_sem, out_sem = scratch[15:]
+    first, bias_v = scratch[12:14]
+    xs_send, xs_recv, pt_send, pt_recv, bd_send, bd_recv, ld_sem = scratch[14:]
 
     dom = lax.axis_index("dom")
     me = lax.axis_index("batch")
@@ -118,7 +119,7 @@
             hand_start(l, 2 * s + direction, piece(l, origin[direction][s], half))
 
     def block(l, j):
-        x = jnp.concatenate([pools[l][codes[l, j, k]] for k in range(FAN)], axis=1)
+        x = jnp.concatenate([pools[l][codes[l, k, j]] for k in range(FAN)], axis=1)
         w = jnp.concatenate([wbufs[l][b, j] for b in range(SHARDS)], axis=0)
         summed = jnp.dot(x, w, preferred_element_type=jnp.float32)
         return jnp.maximum(summed + bias_v[j][l:l + 1], 0.0).astype(jnp.bfloat16)
@@ -144,31 +145,38 @@
         for i in range(NEIGH):
             boundary(l, i).wait_recv()
         if l + 1 < LAYERS:
-            for i in (3, 0, 1, 2):
-                stages[l + 1][i] = block(l, sends[l + 1, 0, i])
+            early = [block(l, sends[l + 1, 0, i]) for i in range(NEIGH)]
+            for i in range(NEIGH):
+                stages[l + 1][i] = early[i]
             boundary_start(l + 1)
 
-            @pl.loop(0, BLK)
-            def _(j):
-                pools[l + 1][j] = block(l, j)
+            @pl.loop(0, BLK // GROUP)
+            def _(g):
+                js = [g * GROUP + u for u in range(GROUP)]
+                values = [block(l, j) for j in js]
+                for j, value in zip(js, values):
+                    pools[l + 1][j] = value
         else:
-            def store(j):
-                columns = pl.ds(pl.multiple_of(j * TILE, TILE), TILE)
-                return pltpu.make_async_copy(final.at[j], out.at[:, columns], out_sem.at[j])
-
-            @pl.loop(0, BLK)
-            def _(j):
-                final[j] = block(l, j)
-
-                @pl.when(j > 0)
-                def _():
-                    store(j - 1).start()
-
-            store(BLK - 1).start()
-            for j in range(BLK):
-                store(j).wait()
+            @pl.loop(0, BLK // GROUP)
+            def _(g):
+                js = [g * GROUP + u for u in range(GROUP)]
+                values = [block(l, j) for j in js]
+                for j, value in zip(js, values):
+                    out[j] = value
+
     for copy in started:
         copy.wait_send()
+
+
+def spread(blocks, out, sem):
+    copies = [
+        pltpu.make_async_copy(blocks.at[j], out.at[:, pl.ds(j * TILE, TILE)], sem.at[j])
+        for j in range(BLK)
+    ]
+    for copy in copies:
+        copy.start()
+    for copy in copies:
+        copy.wait()
 
 
 def body(activations, tile_weights, biases, source_codes, send_list):
@@ -178,28 +186,36 @@
     anywhere = pl.BlockSpec(memory_space=pl.ANY)
     scalars = pl.BlockSpec(memory_space=pltpu.SMEM)
     dma = pltpu.SemaphoreType.DMA
-    return pl.pallas_call(
+    blocks = pl.pallas_call(
         lambda *refs: kernel(parts, rows, *refs),
-        out_shape=jax.ShapeDtypeStruct(activations.shape, jnp.bfloat16),
+        out_shape=pltpu.VMEM((BLK, rows, TILE), jnp.bfloat16),
         in_specs=[anywhere, anywhere, anywhere, scalars, scalars],
-        out_specs=anywhere,
+        out_specs=pl.BlockSpec(memory_space=pltpu.VMEM),
         scratch_shapes=(
             [pltpu.VMEM((SHARDS, BLK, part_rows, TILE), jnp.bfloat16)] * LAYERS
             + [pltpu.VMEM((BLK + NEIGH, rows, TILE), jnp.bfloat16)] * LAYERS
             + [pltpu.VMEM((NEIGH, rows, TILE), jnp.bfloat16)] * LAYERS
             + [
                 pltpu.VMEM((BLK, rows, TILE), jnp.bfloat16),
-                pltpu.VMEM((BLK, rows, TILE), jnp.bfloat16),
                 pltpu.VMEM((BLK, LAYERS, TILE), jnp.float32),
                 dma((LAYERS, 2, 3)), dma((LAYERS, 2, 3)),
                 dma((LAYERS, 7)), dma((LAYERS, 7)),
                 dma((LAYERS, NEIGH)), dma((LAYERS, NEIGH)),
-                dma((3 * BLK + LAYERS,)), dma((BLK,)),
+                dma((3 * BLK + LAYERS,)),
             ]
         ),
         compiler_params=pltpu.CompilerParams(collective_id=0, has_side_effects=True),
         name="layers",
-    )(activations, tile_weights, biases, source_codes, send_list)
+    )(activations, tile_weights, biases, jnp.transpose(source_codes, (0, 2, 1)), send_list)
+    return pl.pallas_call(
+        spread,
+        out_shape=jax.ShapeDtypeStruct(activations.shape, jnp.bfloat16),
+        in_specs=[pl.BlockSpec(memory_space=pltpu.VMEM)],
+        out_specs=anywhere,
+        scratch_shapes=[dma((BLK,))],
+        compiler_params=pltpu.CompilerParams(vmem_limit_bytes=4 << 20),
+        name="spread",
+    )(blocks)
 
 
 def solution(mesh):

time: 66.2 us -> 56.3 us (0.85)
  Pallas kernels: 62.2 us -> 56.1 us
  local copies, waits for them, and re-layouts: 3.71 us -> 0 us
    pallas_call x1 -> x2, Pallas kernels: 62.2 us -> 56.1 us  [the longest x1 55 us: body(): pl.pallas_call(lambda *refs: kernel(parts, rows, *refs), out_shape=pltpu....]
    unnamed x2 -> x0, local copies, waits for them, and re-layouts: 3.71 us -> none
where the time goes in v2:
time: 56.3 us; the launch traced here: 56.1 us
  Pallas kernels  56.1 us (100%)
    pallas_call x1, Pallas kernels, body(): pl.pallas_call(lambda *refs: kernel(parts, rows, *refs), out_shape=pltpu....  55 us

profile of v2, /device:TPU:1, one launch (start us, length us, event | category | flops | bytes accessed | tf_op | source)
XLA Modules:
  0.0 56.1 jit_solution(16218264428408871344)
XLA Ops:
  0.0 55.0 %layers.1.blocks = bf16[16,256,128]{2,1,0:T(8,128)(2,1)S(1)} custom-call(bf16[256,2048]{1,0:T(8,128)(2,1)} %refs_0_.1, bf16[4,16,64,128]{3,2,1,0:T(8,128)(2,1)} %refs_1_.1, f32[4,2048]{1,0:T(4,128)} %refs_2_.1, s32[4,4,16]{2,1,0:T(4,128)} %bitcast.1, s32[4,1,4]{2,1,0:T(1,128)} %refs_4_.1), custom_call_target="tpu_custom_call" | custom-call | tf_op jit(solution)/shard_map/layers/pallas_call | solution.py:189
  55.0 1.1 %spread.1 = bf16[256,2048]{1,0:T(8,128)(2,1)} custom-call(bf16[16,256,128]{2,1,0:T(8,128)(2,1)S(1)} %layers.1.blocks), custom_call_target="tpu_custom_call" | custom-call | tf_op jit(solution)/shard_map/spread/pallas_call | solution.py:210

commit v3 on v2

--- a/solution.py
+++ b/solution.py
@@ -16,7 +16,7 @@
 def kernel(parts, rows, act, weights, biases, codes, sends, out, *scratch):
     wbufs, pools, stages = scratch[0:4], scratch[4:8], scratch[8:12]
     first, bias_v = scratch[12:14]
-    xs_send, xs_recv, pt_send, pt_recv, bd_send, bd_recv, ld_sem = scratch[14:]
+    xs_send, xs_recv, pt_send, pt_recv, bd_send, bd_recv, ld_sem, near, go = scratch[14:]
 
     dom = lax.axis_index("dom")
     me = lax.axis_index("batch")
@@ -27,6 +27,20 @@
     partner = chip * CORES + 1 - core
     offsets = (1, 2, parts - 1, parts // 2)
 
+    barrier = pltpu.get_barrier_semaphore()
+
+    def tell(semaphore, **peer):
+        pl.semaphore_signal(semaphore, inc=1, device_id=peer, device_id_type=MESH)
+
+    @pl.when(core == 0)
+    def _():
+        for peer in (left, right):
+            tell(barrier, batch=peer)
+
+    @pl.when(core == 1)
+    def _():
+        tell(barrier, batch=partner)
+
     loads = []
 
     def load(source, target):
@@ -37,23 +51,6 @@
     load(weights.at[0], wbufs[0].at[me])
     for j in range(BLK):
         load(act.at[:, pl.ds(j * TILE, TILE)], first.at[j])
-    for l in range(1, LAYERS):
-        load(weights.at[l], wbufs[l].at[me])
-    for j in range(BLK):
-        load(biases.at[:, pl.ds(j * TILE, TILE)], bias_v.at[j])
-    for j in range(BLK):
-        load(act.at[:, pl.ds(j * TILE, TILE)], pools[0].at[j])
-
-    barrier = pltpu.get_barrier_semaphore()
-    for peer in (left, right, partner):
-        pl.semaphore_signal(barrier, inc=1, device_id={"batch": peer}, device_id_type=MESH)
-    for offset in offsets:
-        sender = lax.rem(dom + parts - offset, parts)
-        pl.semaphore_signal(barrier, inc=1, device_id={"dom": sender}, device_id_type=MESH)
-    pl.semaphore_wait(barrier, 7)
-
-    started = []
-
     def piece(l, b, h):
         return wbufs[l].at[b, pl.ds(h * HALF, HALF)]
 
@@ -66,9 +63,7 @@
             device_id={"batch": right if direction == 0 else left}, device_id_type=MESH)
 
     def ring_start(l, direction, slot, b):
-        copy = ring(l, direction, slot, b)
-        copy.start()
-        started.append(copy)
+        ring(l, direction, slot, b).start()
 
     origin = ((left, left, far), (right, right, far))
 
@@ -81,9 +76,7 @@
             device_id={"batch": partner}, device_id_type=MESH)
 
     def hand_start(l, slot, ref):
-        copy = hand(l, slot, ref)
-        copy.start()
-        started.append(copy)
+        hand(l, slot, ref).start()
 
     def hand_wait(l):
         for slot in range(6):
@@ -101,9 +94,12 @@
 
     def boundary_start(l):
         for i in (3, 0, 1, 2):
-            copy = boundary(l, i)
-            copy.start()
-            started.append(copy)
+            boundary(l, i).start()
+
+    def ring_own(l):
+        for slot in range(2):
+            for direction in range(2):
+                ring_start(l, direction, slot, me)
 
     def step(l, s):
         for direction in range(2):
@@ -111,9 +107,8 @@
         if s == 0:
             ring_start(l, 0, 2, left)
             ring_start(l, 1, 2, right)
-        elif l + 1 < LAYERS:
-            for direction in range(2):
-                ring_start(l + 1, direction, s - 1, me)
+            if l + 1 < LAYERS:
+                ring_own(l + 1)
         for direction in range(2):
             half = (direction if s != 1 else 1 - direction)
             hand_start(l, 2 * s + direction, piece(l, origin[direction][s], half))
@@ -124,23 +119,67 @@
         summed = jnp.dot(x, w, preferred_element_type=jnp.float32)
         return jnp.maximum(summed + bias_v[j][l:l + 1], 0.0).astype(jnp.bfloat16)
 
-    for copy in loads[:1 + BLK]:
+    loads[0].wait()
+
+    @pl.when(core == 0)
+    def _():
+        pl.semaphore_wait(barrier, 3)
+        for peer in (left, right):
+            tell(near, batch=peer)
+        ring_own(0)
+        hand_start(0, 6, wbufs[0].at[me])
+        pl.semaphore_wait(near, 2)
+        tell(go, batch=partner)
+
+    @pl.when(core == 1)
+    def _():
+        pl.semaphore_wait(go, 1)
+        for offset in offsets:
+            tell(barrier, dom=lax.rem(dom + parts - offset, parts))
+        ring_own(0)
+        hand_start(0, 6, wbufs[0].at[me])
+
+    for copy in loads[1:]:
         copy.wait()
-    for s in range(2):
-        for direction in range(2):
-            ring_start(0, direction, s, me)
-    hand_start(0, 6, wbufs[0].at[me])
+    done = len(loads)
+    for l in range(1, LAYERS):
+        load(weights.at[l], wbufs[l].at[me])
+    for j in range(BLK):
+        load(biases.at[:, pl.ds(j * TILE, TILE)], bias_v.at[j])
+    for j in range(BLK):
+        load(act.at[:, pl.ds(j * TILE, TILE)], pools[0].at[j])
     for i in (3, 0, 1, 2):
         stages[0][i] = first[sends[0, 0, i]]
-    for copy in loads[1 + BLK:]:
+    for copy in loads[done:]:
         copy.wait()
-    boundary_start(0)
     for l in range(1, LAYERS):
         hand_start(l, 6, wbufs[l].at[me])
 
+    soon = dom < parts // 4
+    step(0, 0)
+
+    @pl.when(core == 1)
+    def _():
+        pl.semaphore_wait(barrier, NEIGH)
+        tell(go, batch=partner)
+
+    @pl.when(core == 0)
+    def _():
+        pl.semaphore_wait(go, 1)
+
+    boundary_start(0)
+
     for l in range(LAYERS):
-        for s in range(3):
-            step(l, s)
+        if l > 0:
+            @pl.when(jnp.logical_not(soon))
+            def _():
+                step(l, 0)
+        step(l, 1)
+        step(l, 2)
+        if l + 1 < LAYERS:
+            @pl.when(soon)
+            def _():
+                step(l + 1, 0)
         hand_wait(l)
         for i in range(NEIGH):
             boundary(l, i).wait_recv()
@@ -164,8 +203,18 @@
                 for j, value in zip(js, values):
                     out[j] = value
 
-    for copy in started:
-        copy.wait_send()
+    for l in range(LAYERS):
+        for direction in range(2):
+            for slot in range(3):
+                b = me if slot < 2 else (left, right)[direction]
+                ring(l, direction, slot, b).wait_send()
+        for slot in range(6):
+            direction, s = slot % 2, slot // 2
+            half = (direction if s != 1 else 1 - direction)
+            hand(l, slot, piece(l, origin[direction][s], half)).wait_send()
+        hand(l, 6, wbufs[l].at[me]).wait_send()
+        for i in range(NEIGH):
+            boundary(l, i).wait_send()
 
 
 def spread(blocks, out, sem):
@@ -202,6 +251,7 @@
                 dma((LAYERS, 7)), dma((LAYERS, 7)),
                 dma((LAYERS, NEIGH)), dma((LAYERS, NEIGH)),
                 dma((3 * BLK + LAYERS,)),
+                pltpu.SemaphoreType.REGULAR, pltpu.SemaphoreType.REGULAR,
             ]
         ),
         compiler_params=pltpu.CompilerParams(collective_id=0, has_side_effects=True),

time: 56.3 us -> 54.4 us (0.966); the launches traced: 56.1 us -> 53.6 us
  Pallas kernels: 56.1 us -> 53.6 us
    pallas_call x1, Pallas kernels: 55 us -> 52.5 us  [body(): pl.pallas_call(lambda *refs: kernel(parts, rows, *refs), out_shape=pltpu....]
where the time goes in v3:
time: 54.4 us; the launch traced here: 53.6 us
  Pallas kernels  53.6 us (99%)
    pallas_call x1, Pallas kernels, body(): pl.pallas_call(lambda *refs: kernel(parts, rows, *refs), out_shape=pltpu....  52.5 us
    pallas_call x1, Pallas kernels, body(): pl.pallas_call(spread, out_shape=jax.ShapeDtypeStruct(activations.shape,...  1.09 us

profile of v3, /device:TPU:1, one launch (start us, length us, event | category | flops | bytes accessed | tf_op | source)
XLA Modules:
  0.0 53.6 jit_solution(13834496031335013132)
XLA Ops:
  0.0 52.5 %layers.1.blocks = bf16[16,256,128]{2,1,0:T(8,128)(2,1)S(1)} custom-call(bf16[256,2048]{1,0:T(8,128)(2,1)} %refs_0_.1, bf16[4,16,64,128]{3,2,1,0:T(8,128)(2,1)} %refs_1_.1, f32[4,2048]{1,0:T(4,128)} %refs_2_.1, s32[4,4,16]{2,1,0:T(4,128)} %bitcast.1, s32[4,1,4]{2,1,0:T(1,128)} %refs_4_.1), custom_call_target="tpu_custom_call" | custom-call | tf_op jit(solution)/shard_map/layers/pallas_call | solution.py:238
  52.6 1.1 %spread.1 = bf16[256,2048]{1,0:T(8,128)(2,1)} custom-call(bf16[16,256,128]{2,1,0:T(8,128)(2,1)S(1)} %layers.1.blocks), custom_call_target="tpu_custom_call" | custom-call | tf_op jit(solution)/shard_map/spread/pallas_call | solution.py:260

commit v4 on v3

--- a/solution.py
+++ b/solution.py
@@ -11,12 +11,14 @@
 SHARDS = CHIPS * CORES
 HALF = BLK // 2
 GROUP = 4
+LAST_GROUP = 8
 
 
 def kernel(parts, rows, act, weights, biases, codes, sends, out, *scratch):
-    wbufs, pools, stages = scratch[0:4], scratch[4:8], scratch[8:12]
-    first, bias_v = scratch[12:14]
-    xs_send, xs_recv, pt_send, pt_recv, bd_send, bd_recv, ld_sem, near, go = scratch[14:]
+    wbufs, stages = scratch[0:4], scratch[4:8]
+    pools = [scratch[8:9], scratch[9:10], scratch[10:11], scratch[11:13]]
+    first, bias_v = scratch[13:15]
+    xs_send, xs_recv, pt_send, pt_recv, bd_send, bd_recv, ld_sem, near, go = scratch[15:]
 
     dom = lax.axis_index("dom")
     me = lax.axis_index("batch")
@@ -86,15 +88,27 @@
             hand(l, slot, piece(l, b, half)).wait_recv()
         hand(l, 6, wbufs[l].at[partner]).wait_recv()
 
-    def boundary(l, i):
+    def boundary(l, i, part):
+        count = rows // len(pools[l])
         return pltpu.make_async_remote_copy(
-            src_ref=stages[l].at[i], dst_ref=pools[l].at[BLK + i],
-            send_sem=bd_send.at[l, i], recv_sem=bd_recv.at[l, i],
+            src_ref=stages[l].at[i, pl.ds(part * count, count)], dst_ref=pools[l][part].at[BLK + i],
+            send_sem=bd_send.at[l, i, part], recv_sem=bd_recv.at[l, i, part],
             device_id={"dom": lax.rem(dom + offsets[i], parts)}, device_id_type=MESH)
 
-    def boundary_start(l):
-        for i in (3, 0, 1, 2):
-            boundary(l, i).start()
+    def boundary_start(l, part):
+        @pl.when(last)
+        def _():
+            for i in (0, 1, 3, 2):
+                boundary(l, i, part).start()
+
+        @pl.when(jnp.logical_not(last))
+        def _():
+            for i in (3, 0, 1, 2):
+                boundary(l, i, part).start()
+
+    def boundary_wait(l, part):
+        for i in range(NEIGH):
+            boundary(l, i, part).wait_recv()
 
     def ring_own(l):
         for slot in range(2):
@@ -113,8 +127,9 @@
             half = (direction if s != 1 else 1 - direction)
             hand_start(l, 2 * s + direction, piece(l, origin[direction][s], half))
 
-    def block(l, j):
-        x = jnp.concatenate([pools[l][codes[l, k, j]] for k in range(FAN)], axis=1)
+    def block(l, j, part, start, count):
+        pool = pools[l][part]
+        x = jnp.concatenate([pool[codes[l, k, j], pl.ds(start, count)] for k in range(FAN)], axis=1)
         w = jnp.concatenate([wbufs[l][b, j] for b in range(SHARDS)], axis=0)
         summed = jnp.dot(x, w, preferred_element_type=jnp.float32)
         return jnp.maximum(summed + bias_v[j][l:l + 1], 0.0).astype(jnp.bfloat16)
@@ -147,7 +162,7 @@
     for j in range(BLK):
         load(biases.at[:, pl.ds(j * TILE, TILE)], bias_v.at[j])
     for j in range(BLK):
-        load(act.at[:, pl.ds(j * TILE, TILE)], pools[0].at[j])
+        load(act.at[:, pl.ds(j * TILE, TILE)], pools[0][0].at[j])
     for i in (3, 0, 1, 2):
         stages[0][i] = first[sends[0, 0, i]]
     for copy in loads[done:]:
@@ -156,6 +171,7 @@
         hand_start(l, 6, wbufs[l].at[me])
 
     soon = dom < parts // 4
+    last = dom >= parts - 4
     step(0, 0)
 
     @pl.when(core == 1)
@@ -167,13 +183,9 @@
     def _():
         pl.semaphore_wait(go, 1)
 
-    boundary_start(0)
+    boundary_start(0, 0)
 
     for l in range(LAYERS):
-        if l > 0:
-            @pl.when(jnp.logical_not(soon))
-            def _():
-                step(l, 0)
         step(l, 1)
         step(l, 2)
         if l + 1 < LAYERS:
@@ -181,27 +193,38 @@
             def _():
                 step(l + 1, 0)
         hand_wait(l)
-        for i in range(NEIGH):
-            boundary(l, i).wait_recv()
         if l + 1 < LAYERS:
-            early = [block(l, sends[l + 1, 0, i]) for i in range(NEIGH)]
-            for i in range(NEIGH):
-                stages[l + 1][i] = early[i]
-            boundary_start(l + 1)
+            boundary_wait(l, 0)
+            count = rows // len(pools[l + 1])
+            for part in range(len(pools[l + 1])):
+                early = [block(l, sends[l + 1, 0, i], 0, part * count, count) for i in range(NEIGH)]
+                for i in range(NEIGH):
+                    stages[l + 1][i, pl.ds(part * count, count)] = early[i]
+                boundary_start(l + 1, part)
+
+            @pl.when(jnp.logical_not(soon))
+            def _():
+                step(l + 1, 0)
 
             @pl.loop(0, BLK // GROUP)
             def _(g):
                 js = [g * GROUP + u for u in range(GROUP)]
-                values = [block(l, j) for j in js]
+                values = [block(l, j, 0, 0, rows) for j in js]
                 for j, value in zip(js, values):
-                    pools[l + 1][j] = value
+                    for part in range(len(pools[l + 1])):
+                        pools[l + 1][part][j] = value[part * count:(part + 1) * count]
         else:
-            @pl.loop(0, BLK // GROUP)
-            def _(g):
-                js = [g * GROUP + u for u in range(GROUP)]
-                values = [block(l, j) for j in js]
-                for j, value in zip(js, values):
-                    out[j] = value
+            count = rows // len(pools[l])
+            for part in range(len(pools[l])):
+                boundary_wait(l, part)
+
+                @pl.loop(0, BLK // LAST_GROUP)
+                def _(g):
+                    js = [g * LAST_GROUP + u for u in range(LAST_GROUP)]
+                    values = [block(l, j, part, 0, count) for j in js]
+                    for j, value in zip(js, values):
+                        columns = pl.ds(pl.multiple_of(j * TILE, TILE), TILE)
+                        out[pl.ds(part * count, count), columns] = value
 
     for l in range(LAYERS):
         for direction in range(2):
@@ -213,19 +236,9 @@
             half = (direction if s != 1 else 1 - direction)
             hand(l, slot, piece(l, origin[direction][s], half)).wait_send()
         hand(l, 6, wbufs[l].at[me]).wait_send()
-        for i in range(NEIGH):
-            boundary(l, i).wait_send()
-
-
-def spread(blocks, out, sem):
-    copies = [
-        pltpu.make_async_copy(blocks.at[j], out.at[:, pl.ds(j * TILE, TILE)], sem.at[j])
-        for j in range(BLK)
-    ]
-    for copy in copies:
-        copy.start()
-    for copy in copies:
-        copy.wait()
+        for part in range(len(pools[l])):
+            for i in range(NEIGH):
+                boundary(l, i, part).wait_send()
 
 
 def body(activations, tile_weights, biases, source_codes, send_list):
@@ -235,21 +248,22 @@
     anywhere = pl.BlockSpec(memory_space=pl.ANY)
     scalars = pl.BlockSpec(memory_space=pltpu.SMEM)
     dma = pltpu.SemaphoreType.DMA
-    blocks = pl.pallas_call(
+    return pl.pallas_call(
         lambda *refs: kernel(parts, rows, *refs),
-        out_shape=pltpu.VMEM((BLK, rows, TILE), jnp.bfloat16),
+        out_shape=pltpu.VMEM((rows, BLK * TILE), jnp.bfloat16),
         in_specs=[anywhere, anywhere, anywhere, scalars, scalars],
         out_specs=pl.BlockSpec(memory_space=pltpu.VMEM),
         scratch_shapes=(
             [pltpu.VMEM((SHARDS, BLK, part_rows, TILE), jnp.bfloat16)] * LAYERS
-            + [pltpu.VMEM((BLK + NEIGH, rows, TILE), jnp.bfloat16)] * LAYERS
             + [pltpu.VMEM((NEIGH, rows, TILE), jnp.bfloat16)] * LAYERS
+            + [pltpu.VMEM((BLK + NEIGH, rows, TILE), jnp.bfloat16)] * (LAYERS - 1)
+            + [pltpu.VMEM((BLK + NEIGH, rows // 2, TILE), jnp.bfloat16)] * 2
             + [
                 pltpu.VMEM((BLK, rows, TILE), jnp.bfloat16),
                 pltpu.VMEM((BLK, LAYERS, TILE), jnp.float32),
                 dma((LAYERS, 2, 3)), dma((LAYERS, 2, 3)),
                 dma((LAYERS, 7)), dma((LAYERS, 7)),
-                dma((LAYERS, NEIGH)), dma((LAYERS, NEIGH)),
+                dma((LAYERS, NEIGH, 2)), dma((LAYERS, NEIGH, 2)),
                 dma((3 * BLK + LAYERS,)),
                 pltpu.SemaphoreType.REGULAR, pltpu.SemaphoreType.REGULAR,
             ]
@@ -257,15 +271,6 @@
         compiler_params=pltpu.CompilerParams(collective_id=0, has_side_effects=True),
         name="layers",
     )(activations, tile_weights, biases, jnp.transpose(source_codes, (0, 2, 1)), send_list)
-    return pl.pallas_call(
-        spread,
-        out_shape=jax.ShapeDtypeStruct(activations.shape, jnp.bfloat16),
-        in_specs=[pl.BlockSpec(memory_space=pltpu.VMEM)],
-        out_specs=anywhere,
-        scratch_shapes=[dma((BLK,))],
-        compiler_params=pltpu.CompilerParams(vmem_limit_bytes=4 << 20),
-        name="spread",
-    )(blocks)
 
 
 def solution(mesh):

time: 54.4 us -> 51.9 us (0.954)
  Pallas kernels: 53.6 us -> 50.3 us
  local copies, waits for them, and re-layouts: 0 us -> 0.97 us
    pallas_call x1, Pallas kernels: 52.5 us -> 50.3 us  [body(): pl.pallas_call(lambda *refs: kernel(parts, rows, *refs), out_shape=pltpu....]
    pallas_call x1 -> x0, Pallas kernels: 1.09 us -> none  [body(): pl.pallas_call(spread, out_shape=jax.ShapeDtypeStruct(activations.shape,...]
    unnamed x0 -> x1, local copies, waits for them, and re-layouts: none -> 0.97 us
where the time goes in v4:
time: 51.9 us; the launch traced here: 51.3 us
  Pallas kernels  50.3 us (97%)
  local copies, waits for them, and re-layouts  0.97 us (2%)
    pallas_call x1, Pallas kernels, body(): pl.pallas_call(lambda *refs: kernel(parts, rows, *refs), out_shape=pltpu....  50.3 us

profile of v4, /device:TPU:1, one launch (start us, length us, event | category | flops | bytes accessed | tf_op | source)
XLA Modules:
  0.0 51.3 jit_solution(12825588425443355781)
XLA Ops:
  0.0 50.3 %layers.1 = bf16[256,2048]{1,0:T(8,128)(2,1)S(1)} custom-call(bf16[256,2048]{1,0:T(8,128)(2,1)} %refs_0_.1, bf16[4,16,64,128]{3,2,1,0:T(8,128)(2,1)} %refs_1_.1, f32[4,2048]{1,0:T(4,128)} %refs_2_.1, s32[4,4,16]{2,1,0:T(4,128)} %bitcast.1, s32[4,1,4]{2,1,0:T(1,128)} %refs_4_.1), custom_call_target="tpu_custom_call" | custom-call | tf_op jit(solution)/shard_map/layers/pallas_call | solution.py:251
  50.3 1.0 %copy.7 = bf16[256,2048]{1,0:T(8,128)(2,1)} copy(bf16[256,2048]{1,0:T(8,128)(2,1)S(1)} %layers.1) | data formatting | bytes 2097152

commit v5 on v4

--- a/solution.py
+++ b/solution.py
@@ -14,11 +14,11 @@
 LAST_GROUP = 8
 
 
-def kernel(parts, rows, act, weights, biases, codes, sends, out, *scratch):
+def kernel(parts, rows, act, weights, biases, codes_in, sends_in, out, *scratch):
     wbufs, stages = scratch[0:4], scratch[4:8]
     pools = [scratch[8:9], scratch[9:10], scratch[10:11], scratch[11:13]]
     first, bias_v = scratch[13:15]
-    xs_send, xs_recv, pt_send, pt_recv, bd_send, bd_recv, ld_sem, near, go = scratch[15:]
+    xs_send, xs_recv, pt_send, pt_recv, bd_send, bd_recv, ld_sem, near, go, codes, sends = scratch[15:]
 
     dom = lax.axis_index("dom")
     me = lax.axis_index("batch")
@@ -51,6 +51,8 @@
         loads.append(copy)
 
     load(weights.at[0], wbufs[0].at[me])
+    load(codes_in, codes)
+    load(sends_in, sends)
     for j in range(BLK):
         load(act.at[:, pl.ds(j * TILE, TILE)], first.at[j])
     def piece(l, b, h):
@@ -246,12 +248,11 @@
     parts = lax.axis_size("dom")
     part_rows = FAN * TILE // SHARDS
     anywhere = pl.BlockSpec(memory_space=pl.ANY)
-    scalars = pl.BlockSpec(memory_space=pltpu.SMEM)
     dma = pltpu.SemaphoreType.DMA
     return pl.pallas_call(
         lambda *refs: kernel(parts, rows, *refs),
         out_shape=pltpu.VMEM((rows, BLK * TILE), jnp.bfloat16),
-        in_specs=[anywhere, anywhere, anywhere, scalars, scalars],
+        in_specs=[anywhere] * 5,
         out_specs=pl.BlockSpec(memory_space=pltpu.VMEM),
         scratch_shapes=(
             [pltpu.VMEM((SHARDS, BLK, part_rows, TILE), jnp.bfloat16)] * LAYERS
@@ -264,8 +265,9 @@
                 dma((LAYERS, 2, 3)), dma((LAYERS, 2, 3)),
                 dma((LAYERS, 7)), dma((LAYERS, 7)),
                 dma((LAYERS, NEIGH, 2)), dma((LAYERS, NEIGH, 2)),
-                dma((3 * BLK + LAYERS,)),
+                dma((3 * BLK + LAYERS + 2,)),
                 pltpu.SemaphoreType.REGULAR, pltpu.SemaphoreType.REGULAR,
+                pltpu.SMEM(source_codes.shape[:1] + source_codes.shape[:0:-1], jnp.int32), pltpu.SMEM(send_list.shape, jnp.int32),
             ]
         ),
         compiler_params=pltpu.CompilerParams(collective_id=0, has_side_effects=True),

time: 51.9 us -> 51 us (0.983)
  Pallas kernels: 50.3 us -> 49.4 us
    pallas_call x1, Pallas kernels: 50.3 us -> 49.4 us  [body(): pl.pallas_call(lambda *refs: kernel(parts, rows, *refs), out_shape=pltpu....]
where the time goes in v5:
time: 51 us; the launch traced here: 50.4 us
  Pallas kernels  49.4 us (97%)
  local copies, waits for them, and re-layouts  0.97 us (2%)
    pallas_call x1, Pallas kernels, body(): pl.pallas_call(lambda *refs: kernel(parts, rows, *refs), out_shape=pltpu....  49.4 us

profile of v5, /device:TPU:1, one launch (start us, length us, event | category | flops | bytes accessed | tf_op | source)
XLA Modules:
  0.0 50.4 jit_solution(16703127646957645765)
XLA Ops:
  0.0 49.4 %layers.1 = bf16[256,2048]{1,0:T(8,128)(2,1)S(1)} custom-call(bf16[256,2048]{1,0:T(8,128)(2,1)} %refs_0_.1, bf16[4,16,64,128]{3,2,1,0:T(8,128)(2,1)} %refs_1_.1, f32[4,2048]{1,0:T(4,128)} %refs_2_.1, s32[4,4,16]{2,1,0:T(4,128)} %bitcast.1, s32[4,1,4]{2,1,0:T(1,128)} %refs_4_.1), custom_call_target="tpu_custom_call" | custom-call | tf_op jit(solution)/shard_map/layers/pallas_call | solution.py:252
  49.4 1.0 %copy.7 = bf16[256,2048]{1,0:T(8,128)(2,1)} copy(bf16[256,2048]{1,0:T(8,128)(2,1)S(1)} %layers.1) | data formatting | bytes 2097152

commit v6 on v5

--- a/solution.py
+++ b/solution.py
@@ -135,6 +135,20 @@
         w = jnp.concatenate([wbufs[l][b, j] for b in range(SHARDS)], axis=0)
         summed = jnp.dot(x, w, preferred_element_type=jnp.float32)
         return jnp.maximum(summed + bias_v[j][l:l + 1], 0.0).astype(jnp.bfloat16)
+
+    def sent(l):
+        for direction in range(2):
+            for slot in range(3):
+                b = me if slot < 2 else (left, right)[direction]
+                ring(l, direction, slot, b).wait_send()
+        for slot in range(6):
+            direction, s = slot % 2, slot // 2
+            half = (direction if s != 1 else 1 - direction)
+            hand(l, slot, piece(l, origin[direction][s], half)).wait_send()
+        hand(l, 6, wbufs[l].at[me]).wait_send()
+        for part in range(len(pools[l])):
+            for i in range(NEIGH):
+                boundary(l, i, part).wait_send()
 
     loads[0].wait()
 
@@ -217,6 +231,8 @@
                         pools[l + 1][part][j] = value[part * count:(part + 1) * count]
         else:
             count = rows // len(pools[l])
+            for layer in range(LAYERS - 1):
+                sent(layer)
             for part in range(len(pools[l])):
                 boundary_wait(l, part)
 
@@ -227,20 +243,7 @@
                     for j, value in zip(js, values):
                         columns = pl.ds(pl.multiple_of(j * TILE, TILE), TILE)
                         out[pl.ds(part * count, count), columns] = value
-
-    for l in range(LAYERS):
-        for direction in range(2):
-            for slot in range(3):
-                b = me if slot < 2 else (left, right)[direction]
-                ring(l, direction, slot, b).wait_send()
-        for slot in range(6):
-            direction, s = slot % 2, slot // 2
-            half = (direction if s != 1 else 1 - direction)
-            hand(l, slot, piece(l, origin[direction][s], half)).wait_send()
-        hand(l, 6, wbufs[l].at[me]).wait_send()
-        for part in range(len(pools[l])):
-            for i in range(NEIGH):
-                boundary(l, i, part).wait_send()
+    sent(LAYERS - 1)
 
 
 def body(activations, tile_weights, biases, source_codes, send_list):

time: 51 us -> 50.9 us (level)
  no operation moved by 1% of the time
where the time goes in v6:
time: 50.9 us; the launch traced here: 50.3 us
  Pallas kernels  49.3 us (97%)
  local copies, waits for them, and re-layouts  0.97 us (2%)
    pallas_call x1, Pallas kernels, body(): pl.pallas_call(lambda *refs: kernel(parts, rows, *refs), out_shape=pltpu....  49.3 us

profile of v6, /device:TPU:1, one launch (start us, length us, event | category | flops | bytes accessed | tf_op | source)
XLA Modules:
  0.0 50.3 jit_solution(10116820150249742994)
XLA Ops:
  0.0 49.3 %layers.1 = bf16[256,2048]{1,0:T(8,128)(2,1)S(1)} custom-call(bf16[256,2048]{1,0:T(8,128)(2,1)} %refs_0_.1, bf16[4,16,64,128]{3,2,1,0:T(8,128)(2,1)} %refs_1_.1, f32[4,2048]{1,0:T(4,128)} %refs_2_.1, s32[4,4,16]{2,1,0:T(4,128)} %bitcast.1, s32[4,1,4]{2,1,0:T(1,128)} %refs_4_.1), custom_call_target="tpu_custom_call" | custom-call | tf_op jit(solution)/shard_map/layers/pallas_call | solution.py:255
  49.3 1.0 %copy.7 = bf16[256,2048]{1,0:T(8,128)(2,1)} copy(bf16[256,2048]{1,0:T(8,128)(2,1)S(1)} %layers.1) | data formatting | bytes 2097152

commit v7 on v6

--- a/solution.py
+++ b/solution.py
@@ -10,8 +10,10 @@
 CHIPS, CORES = 4, 2
 SHARDS = CHIPS * CORES
 HALF = BLK // 2
+SUBS = 2
+SLOTS = 2 + SUBS
 GROUP = 4
-LAST_GROUP = 8
+LAST_GROUP = 16
 
 
 def kernel(parts, rows, act, weights, biases, codes_in, sends_in, out, *scratch):
@@ -55,40 +57,39 @@
     load(sends_in, sends)
     for j in range(BLK):
         load(act.at[:, pl.ds(j * TILE, TILE)], first.at[j])
-    def piece(l, b, h):
-        return wbufs[l].at[b, pl.ds(h * HALF, HALF)]
+
+    def piece(l, direction, slot, b):
+        begin = (direction if slot != 1 else 1 - direction) * HALF
+        count = HALF
+        if slot > 1:
+            count = HALF // SUBS
+            begin = begin + (slot - 2) * count
+        return wbufs[l].at[b, pl.ds(begin, count)]
 
     def ring(l, direction, slot, b):
-        half = (direction if slot != 1 else 1 - direction)
-        ref = piece(l, b, half)
+        ref = piece(l, direction, slot, b)
         return pltpu.make_async_remote_copy(
             src_ref=ref, dst_ref=ref,
             send_sem=xs_send.at[l, direction, slot], recv_sem=xs_recv.at[l, direction, slot],
             device_id={"batch": right if direction == 0 else left}, device_id_type=MESH)
 
-    def ring_start(l, direction, slot, b):
-        ring(l, direction, slot, b).start()
-
-    origin = ((left, left, far), (right, right, far))
-
-    def ring_wait(l, direction, slot):
-        ring(l, direction, slot, origin[direction][slot]).wait_recv()
+    def origin(direction, slot):
+        return (left, right)[direction] if slot < 2 else far
 
     def hand(l, slot, ref):
         return pltpu.make_async_remote_copy(
             src_ref=ref, dst_ref=ref, send_sem=pt_send.at[l, slot], recv_sem=pt_recv.at[l, slot],
             device_id={"batch": partner}, device_id_type=MESH)
 
-    def hand_start(l, slot, ref):
-        hand(l, slot, ref).start()
-
     def hand_wait(l):
-        for slot in range(6):
-            direction, s = slot % 2, slot // 2
-            half = (direction if s != 1 else 1 - direction)
-            b = origin[direction][s] + 1 - 2 * core
-            hand(l, slot, piece(l, b, half)).wait_recv()
-        hand(l, 6, wbufs[l].at[partner]).wait_recv()
+        for slot in range(SLOTS):
+            for direction in range(2):
+                b = origin(direction, slot) + 1 - 2 * core
+                hand(l, 2 * slot + direction, piece(l, direction, slot, b)).wait_recv()
+        hand(l, 2 * SLOTS, wbufs[l].at[partner]).wait_recv()
+
+    def hand_own(l):
+        return hand(l, 2 * SLOTS, wbufs[l].at[me])
 
     def boundary(l, i, part):
         count = rows // len(pools[l])
@@ -115,19 +116,21 @@
     def ring_own(l):
         for slot in range(2):
             for direction in range(2):
-                ring_start(l, direction, slot, me)
+                ring(l, direction, slot, me).start()
 
     def step(l, s):
-        for direction in range(2):
-            ring_wait(l, direction, s)
-        if s == 0:
-            ring_start(l, 0, 2, left)
-            ring_start(l, 1, 2, right)
-            if l + 1 < LAYERS:
-                ring_own(l + 1)
-        for direction in range(2):
-            half = (direction if s != 1 else 1 - direction)
-            hand_start(l, 2 * s + direction, piece(l, origin[direction][s], half))
+        for slot in (range(2, SLOTS) if s == 2 else (s,)):
+            for direction in range(2):
+                ring(l, direction, slot, origin(direction, slot)).wait_recv()
+            if s == 0:
+                for onward in range(2, SLOTS):
+                    for direction in range(2):
+                        ring(l, direction, onward, origin(direction, slot)).start()
+                if l + 1 < LAYERS:
+                    ring_own(l + 1)
+            for direction in range(2):
+                b = origin(direction, slot)
+                hand(l, 2 * slot + direction, piece(l, direction, slot, b)).start()
 
     def block(l, j, part, start, count):
         pool = pools[l][part]
@@ -137,15 +140,11 @@
         return jnp.maximum(summed + bias_v[j][l:l + 1], 0.0).astype(jnp.bfloat16)
 
     def sent(l):
-        for direction in range(2):
-            for slot in range(3):
-                b = me if slot < 2 else (left, right)[direction]
-                ring(l, direction, slot, b).wait_send()
-        for slot in range(6):
-            direction, s = slot % 2, slot // 2
-            half = (direction if s != 1 else 1 - direction)
-            hand(l, slot, piece(l, origin[direction][s], half)).wait_send()
-        hand(l, 6, wbufs[l].at[me]).wait_send()
+        for slot in range(SLOTS):
+            for direction in range(2):
+                ring(l, direction, slot, me if slot < 2 else (left, right)[direction]).wait_send()
+                hand(l, 2 * slot + direction, piece(l, direction, slot, origin(direction, slot))).wait_send()
+        hand_own(l).wait_send()
         for part in range(len(pools[l])):
             for i in range(NEIGH):
                 boundary(l, i, part).wait_send()
@@ -158,7 +157,7 @@
         for peer in (left, right):
             tell(near, batch=peer)
         ring_own(0)
-        hand_start(0, 6, wbufs[0].at[me])
+        hand_own(0).start()
         pl.semaphore_wait(near, 2)
         tell(go, batch=partner)
 
@@ -168,7 +167,7 @@
         for offset in offsets:
             tell(barrier, dom=lax.rem(dom + parts - offset, parts))
         ring_own(0)
-        hand_start(0, 6, wbufs[0].at[me])
+        hand_own(0).start()
 
     for copy in loads[1:]:
         copy.wait()
@@ -183,12 +182,13 @@
         stages[0][i] = first[sends[0, 0, i]]
     for copy in loads[done:]:
         copy.wait()
-    for l in range(1, LAYERS):
-        hand_start(l, 6, wbufs[l].at[me])
 
     soon = dom < parts // 4
     last = dom >= parts - 4
-    step(0, 0)
+
+    @pl.when(soon)
+    def _():
+        step(0, 0)
 
     @pl.when(core == 1)
     def _():
@@ -200,6 +200,12 @@
         pl.semaphore_wait(go, 1)
 
     boundary_start(0, 0)
+    for l in range(1, LAYERS):
+        hand_own(l).start()
+
+    @pl.when(jnp.logical_not(soon))
+    def _():
+        step(0, 0)
 
     for l in range(LAYERS):
         step(l, 1)
@@ -265,8 +271,8 @@
             + [
                 pltpu.VMEM((BLK, rows, TILE), jnp.bfloat16),
                 pltpu.VMEM((BLK, LAYERS, TILE), jnp.float32),
-                dma((LAYERS, 2, 3)), dma((LAYERS, 2, 3)),
-                dma((LAYERS, 7)), dma((LAYERS, 7)),
+                dma((LAYERS, 2, SLOTS)), dma((LAYERS, 2, SLOTS)),
+                dma((LAYERS, 2 * SLOTS + 1)), dma((LAYERS, 2 * SLOTS + 1)),
                 dma((LAYERS, NEIGH, 2)), dma((LAYERS, NEIGH, 2)),
                 dma((3 * BLK + LAYERS + 2,)),
                 pltpu.SemaphoreType.REGULAR, pltpu.SemaphoreType.REGULAR,

time: 50.9 us -> 50 us (0.982)
  Pallas kernels: 49.3 us -> 48.5 us
    pallas_call x1, Pallas kernels: 49.3 us -> 48.5 us  [body(): pl.pallas_call(lambda *refs: kernel(parts, rows, *refs), out_shape=pltpu....]
where the time goes in v7:
time: 50 us; the launch traced here: 49.5 us
  Pallas kernels  48.5 us (97%)
  local copies, waits for them, and re-layouts  0.97 us (2%)
    pallas_call x1, Pallas kernels, body(): pl.pallas_call(lambda *refs: kernel(parts, rows, *refs), out_shape=pltpu....  48.5 us

profile of v7, /device:TPU:1, one launch (start us, length us, event | category | flops | bytes accessed | tf_op | source)
XLA Modules:
  0.0 49.5 jit_solution(18305209042851875141)
XLA Ops:
  0.0 48.5 %layers.1 = bf16[256,2048]{1,0:T(8,128)(2,1)S(1)} custom-call(bf16[256,2048]{1,0:T(8,128)(2,1)} %refs_0_.1, bf16[4,16,64,128]{3,2,1,0:T(8,128)(2,1)} %refs_1_.1, f32[4,2048]{1,0:T(4,128)} %refs_2_.1, s32[4,4,16]{2,1,0:T(4,128)} %bitcast.1, s32[4,1,4]{2,1,0:T(1,128)} %refs_4_.1), custom_call_target="tpu_custom_call" | custom-call | tf_op jit(solution)/shard_map/layers/pallas_call | solution.py:261
  48.5 1.0 %copy.7 = bf16[256,2048]{1,0:T(8,128)(2,1)} copy(bf16[256,2048]{1,0:T(8,128)(2,1)S(1)} %layers.1) | data formatting | bytes 2097152

commit v8 on v7

--- a/solution.py
+++ b/solution.py
@@ -101,12 +101,12 @@
     def boundary_start(l, part):
         @pl.when(last)
         def _():
-            for i in (0, 1, 3, 2):
+            for i in (1, 0, 3, 2):
                 boundary(l, i, part).start()
 
         @pl.when(jnp.logical_not(last))
         def _():
-            for i in (3, 0, 1, 2):
+            for i in ((3, 0, 1, 2) if part == 0 else (1, 0, 3, 2)):
                 boundary(l, i, part).start()
 
     def boundary_wait(l, part):
@@ -157,16 +157,16 @@
         for peer in (left, right):
             tell(near, batch=peer)
         ring_own(0)
-        hand_own(0).start()
         pl.semaphore_wait(near, 2)
         tell(go, batch=partner)
+        hand_own(0).start()
 
     @pl.when(core == 1)
     def _():
         pl.semaphore_wait(go, 1)
+        ring_own(0)
         for offset in offsets:
             tell(barrier, dom=lax.rem(dom + parts - offset, parts))
-        ring_own(0)
         hand_own(0).start()
 
     for copy in loads[1:]:

time: 50 us -> 49.6 us (level)
  no operation moved by 1% of the time
where the time goes in v8:
time: 49.6 us; the launch traced here: 49.5 us
  Pallas kernels  48.5 us (98%)
  local copies, waits for them, and re-layouts  0.97 us (2%)
    pallas_call x1, Pallas kernels, body(): pl.pallas_call(lambda *refs: kernel(parts, rows, *refs), out_shape=pltpu....  48.5 us

profile of v8, /device:TPU:1, one launch (start us, length us, event | category | flops | bytes accessed | tf_op | source)
XLA Modules:
  0.0 49.5 jit_solution(5265782750670696765)
XLA Ops:
  0.0 48.5 %layers.1 = bf16[256,2048]{1,0:T(8,128)(2,1)S(1)} custom-call(bf16[256,2048]{1,0:T(8,128)(2,1)} %refs_0_.1, bf16[4,16,64,128]{3,2,1,0:T(8,128)(2,1)} %refs_1_.1, f32[4,2048]{1,0:T(4,128)} %refs_2_.1, s32[4,4,16]{2,1,0:T(4,128)} %bitcast.1, s32[4,1,4]{2,1,0:T(1,128)} %refs_4_.1), custom_call_target="tpu_custom_call" | custom-call | tf_op jit(solution)/shard_map/layers/pallas_call | solution.py:261
  48.5 1.0 %copy.7 = bf16[256,2048]{1,0:T(8,128)(2,1)} copy(bf16[256,2048]{1,0:T(8,128)(2,1)S(1)} %layers.1) | data formatting | bytes 2097152
